TPU v7x, 256 devices: a whole 4x4x8 slice. The times are simulated.
256 devices in a mesh: rep: 4 (over x_hi, core), tp: 32 (over z, y), dec: 2 (over x_lo).
Axes of the slice: x: 4 (x_hi: 2, x_lo: 2; x = x_hi * 2 + x_lo), y: 4, z: 8, core: 2. Of those that a mesh axis runs over, the one named last changes fastest.
Arguments:
- residual: bfloat16 [4096, 4096], P(('rep', 'tp', 'dec')), may hold values from -6 to 6
- queries: bfloat16 [128, 2, 16, 4096], P('rep', 'dec', None, 'tp'), may hold values from -64 to 64
- kv_pool: bfloat16 [256, 8, 128, 256], P(('rep', 'tp', 'dec')), may hold values from -8 to 8
- prior_len: int32 [16], P('rep'), may hold values from 0 to 1792, as said below
- page_table: int32 [16, 16], P('rep'), may hold values from -1 to 255, as said below
- page_target: int32 [256], P(('rep', 'tp', 'dec')), may hold values from 0 to 3, as said below
- out_weight: bfloat16 [4096, 4096], P('tp'), may hold values from -0.5 to 0.5
- moe_gain: float32 [4096], replicated, may hold values from 0.1 to 1.9
- expert_ids: int32 [4096, 2], P(('rep', 'tp', 'dec')), may hold values from 0 to 7, as said below
- expert_gates: float32 [4096, 2], P(('rep', 'tp', 'dec')), may hold values from 0.1 to 1
- w_gate: bfloat16 [2, 14336, 4096], P('dec', 'tp'), may hold values from -0.09375 to 0.09375
- w_up: bfloat16 [2, 14336, 4096], P('dec', 'tp'), may hold values from -0.09375 to 0.09375
- w_down: bfloat16 [2, 14336, 4096], P('dec', 'tp'), may hold values from -0.1875 to 0.1875
Outputs:
- layer_out: bfloat16 [4096, 4096], P(('rep', 'tp', 'dec'))
- decode_pages: bfloat16 [256, 8, 128, 256], P(('rep', 'tp', 'dec'))
Inputs may be any that keep to these rules, and one draw needn't show every extreme that they name: `prior_len`: each value is a multiple of 256; in every rep index's 4 requests one request has the largest value. `page_table`: for request q, the first (prior_len[q] + 256) // 128 entries are distinct slots among the 64 slots of q's rep index (slots r * 64 to r * 64 + 63), no slot named twice in a rep index; the other entries are -1. Slots that no entry names hold data that attention never reads. `page_target`: for every m, the slots r * 64 + m over all rep indices r go to distinct rep indices. `expert_ids`: each row names two different experts; among the 16 rows of each device (aligned blocks of rows) every expert is named by exactly 4 rows.
All inputs are finite; a program needn't handle non-finite values.
Results may differ from a plain program's by a relative error of at most 0.02.
Values may be sent and summed in bfloat16 or wider, within the bound.
A program may use at most 64 MiB of HBM per device.

v0:
```python
import jax
import jax.numpy as jnp
from jax import lax
from jax.sharding import PartitionSpec as P

QH = 32
KVH = 8
EXPERTS = 8
TOPK = 2
EXP_WIN = 2


def hand_over(kv_pool, page_target):
    rep_size = lax.axis_size("rep")
    owners = jnp.arange(rep_size, dtype=jnp.int32)
    selected = (page_target[None, :] == owners[:, None])[:, :, None, None, None]
    outgoing = jnp.where(selected, kv_pool[None], jnp.zeros((), kv_pool.dtype))
    incoming = lax.all_to_all(outgoing, "rep", split_axis=0, concat_axis=0, tiled=True)
    return jnp.sum(incoming, axis=0)


def on_device(
    residual,
    queries,
    kv_pool,
    prior_len,
    page_table,
    page_target,
    out_weight,
    moe_gain,
    expert_ids,
    expert_gates,
    w_gate,
    w_up,
    w_down,
):
    tp_size = lax.axis_size("tp")
    dec_size = lax.axis_size("dec")
    dec_index = lax.axis_index("dec")
    slots_dev, kv_heads, page_rows, both_dim = kv_pool.shape
    head_dim = both_dim // 2
    heads_dev = queries.shape[3] // head_dim
    group_size = QH // KVH
    kv_dev = max(1, heads_dev // group_size)
    copies = max(1, group_size // heads_dev)
    per_kv = heads_dev // kv_dev
    requests = prior_len.shape[0]
    tok_dev = queries.shape[2]
    half_rows = queries.shape[0] * tok_dev // requests
    pages_max = page_table.shape[1]
    team_size = tp_size * dec_size
    spread = jnp.repeat(kv_pool, copies, axis=1).reshape(
        slots_dev, tp_size, kv_dev, page_rows, both_dim
    )
    holder = page_table // slots_dev % team_size
    number = page_table % slots_dev
    outgoing = jnp.broadcast_to(
        spread[:, :, None], (slots_dev, tp_size, dec_size, kv_dev, page_rows, both_dim)
    )
    outgoing = outgoing.reshape(slots_dev, team_size, kv_dev, page_rows, both_dim)
    received = lax.all_to_all(outgoing, ("tp", "dec"), split_axis=1, concat_axis=0, tiled=True)
    local_index = holder * slots_dev + number
    received = received.reshape(team_size * slots_dev, kv_dev, page_rows, both_dim)
    gathered_pages = received[local_index]
    keys_part = gathered_pages[..., :head_dim]
    values_part = gathered_pages[..., head_dim:]
    query_rows = queries.reshape(requests, half_rows, kv_dev, per_kv, head_dim)
    key_count = pages_max * page_rows
    scores = jnp.einsum(
        "rukgd,rpkwd->rukgpw", query_rows, keys_part, preferred_element_type=jnp.float32
    )
    scores = scores.reshape(requests, half_rows, kv_dev, per_kv, key_count) * head_dim ** (-0.5)
    position = jnp.arange(key_count, dtype=jnp.int32)
    local_row = jnp.arange(half_rows, dtype=jnp.int32)
    offset = (local_row // tok_dev * dec_size + dec_index) * tok_dev + local_row % tok_dev
    last_seen = prior_len[:, None] + offset[None, :]
    visible = (position[None, None, :] <= last_seen[:, :, None])[:, :, None, None, :]
    scores = jnp.where(visible, scores, -1e30)
    row_top = jnp.max(scores, axis=-1, keepdims=True)
    raw_weights = jnp.where(visible, jnp.exp(scores - row_top), 0.0)
    totals = jnp.sum(raw_weights, axis=-1)
    weights_low = raw_weights.astype(jnp.bfloat16).reshape(
        requests, half_rows, kv_dev, per_kv, pages_max, page_rows
    )
    weighted = jnp.einsum(
        "rukgpw,rpkwd->rukgd", weights_low, values_part, preferred_element_type=jnp.float32
    )
    attended = (
        (weighted / totals[..., None])
        .astype(jnp.bfloat16)
        .reshape(requests * half_rows, heads_dev * head_dim)
    )
    projected = lax.psum_scatter(
        jnp.dot(attended, out_weight, preferred_element_type=jnp.float32).astype(jnp.bfloat16),
        "tp",
        scatter_dimension=0,
        tiled=True,
    ).astype(jnp.float32)
    mid_state = residual.astype(jnp.float32) + projected
    routed_dev = tok_dev * TOPK // EXPERTS
    row_lists = []
    gate_lists = []
    for expert in range(EXP_WIN):
        names_it = expert_ids == expert
        chosen_rows = jnp.nonzero(jnp.any(names_it, axis=-1), size=routed_dev)[0].astype(jnp.int32)
        row_lists.append(chosen_rows)
        gate_lists.append(jnp.sum(jnp.where(names_it, expert_gates, 0.0), axis=-1)[chosen_rows])
    picked_rows = jnp.stack(row_lists, axis=1)
    picked_gates = jnp.stack(gate_lists, axis=1)
    selected = mid_state[picked_rows]
    inverse = lax.rsqrt(jnp.mean(selected * selected, axis=-1, keepdims=True) + 1e-05)
    normed = (selected * inverse * moe_gain).astype(jnp.bfloat16)
    exp_dec = w_gate.shape[0]
    width = normed.shape[2]
    by_expert = normed.reshape(routed_dev, dec_size, exp_dec, width)
    row_piece = lax.dynamic_index_in_dim(
        lax.all_gather(by_expert, ("tp", "dec"), axis=0, tiled=True), dec_index, 1, keepdims=False
    )
    gate_part = jnp.einsum("ned,efd->nef", row_piece, w_gate, preferred_element_type=jnp.float32)
    up_part = jnp.einsum("ned,efd->nef", row_piece, w_up, preferred_element_type=jnp.float32)
    hidden = (jax.nn.silu(gate_part) * up_part).astype(jnp.bfloat16)
    expert_part = lax.psum_scatter(
        jnp.einsum("nef,efd->ned", hidden, w_down, preferred_element_type=jnp.float32).astype(
            jnp.bfloat16
        ),
        "tp",
        scatter_dimension=0,
        tiled=True,
    ).astype(jnp.float32)
    expert_part = expert_part.reshape(dec_size, routed_dev, exp_dec, width)
    expert_out = (
        lax.all_to_all(
            expert_part.astype(jnp.bfloat16), "dec", split_axis=0, concat_axis=2, tiled=True
        )
        .astype(expert_part.dtype)
        .reshape(routed_dev, dec_size * exp_dec, width)
    )
    mixture = jnp.zeros_like(mid_state)
    for expert in range(EXP_WIN):
        mixture = mixture.at[picked_rows[:, expert]].add(
            expert_out[:, expert] * picked_gates[:, expert][:, None]
        )
    layer_out = (mid_state + mixture).astype(jnp.bfloat16)
    decode_pages = hand_over(kv_pool, page_target)
    return (layer_out, decode_pages)


def solution(mesh):
    return jax.shard_map(
        on_device,
        mesh=mesh,
        in_specs=(
            P(("rep", "tp", "dec"), None),
            P("rep", "dec", None, "tp"),
            P(("rep", "tp", "dec"), None, None, None),
            P("rep"),
            P("rep", None),
            P(("rep", "tp", "dec")),
            P("tp", None),
            P(),
            P(("rep", "tp", "dec"), None),
            P(("rep", "tp", "dec"), None),
            P("dec", "tp", None),
            P("dec", "tp", None),
            P("dec", "tp", None),
        ),
        out_specs=(P(("rep", "tp", "dec"), None), P(("rep", "tp", "dec"), None, None, None)),
        check_vma=False,
    )
```

profile of v0, /device:TPU:4, one launch (start us, length us, event | category | flops | bytes accessed | tf_op | source)
XLA Modules:
  0.0 915.2 jit_solution(17047965572777546698)
XLA Ops:
  7.2 1.4 broadcast_in_dim.77
  8.5 2.7 broadcast_in_dim.79
  11.2 13.1 %all-to-all-start = ((bf16[1,64,1,128,256]{4,3,2,0,1:T(8,128)(2,1)}), bf16[1,64,1,128,256]{4,3,2,0,1:T(8,128)(2,1)}, u32[]{:S(2)}, u32[]{:S(2)}) async-start(bf16[1,64,1,128,256]{4,3,2,0,1:T(8,128)(2,1)} %bitcast.171), calls=%async_computation | async-start | bytes 8388608 | tf_op jit(solution)/shard_map/all_to_all | solution.py:61
  24.6 95.0 %all-to-all-done = bf16[1,64,1,128,256]{4,3,2,0,1:T(8,128)(2,1)} async-done(((bf16[1,64,1,128,256]{4,3,2,0,1:T(8,128)(2,1)}), bf16[1,64,1,128,256]{4,3,2,0,1:T(8,128)(2,1)}, u32[]{:S(2)}, u32[]{:S(2)}) %all-to-all-start) | async-done | bytes 4194336 | tf_op jit(solution)/shard_map/all_to_all | solution.py:61
  119.6 5.0 gather_fusion
  124.6 2.4 fusion.6
  127.0 1.3 fusion.7
  128.3 1.7 fusion.39
  130.1 3.2 convolution_convert_fusion
  137.7 214.3 %reduce-scatter.3.cloned.1.call-done = bf16[16,4096]{1,0:T(8,128)(2,1)} async-done(((bf16[512,4096]{1,0:T(8,128)(2,1)}), bf16[16,4096]{1,0:T(8,128)(2,1)}) %reduce-scatter.3.cloned.1.call-update) | async-done | bytes 131088 | tf_op jit(solution)/shard_map/reduce_scatter | solution.py:93
  352.0 0.9 convert_add_fusion
  354.9 302.4 %all-gather.2.cloned.1.call-done = bf16[256,2,1,4096]{3,1,2,0:T(2,128)(2,1)} async-done(((bf16[4,2,1,4096]{3,1,2,0:T(2,128)(2,1)}), bf16[256,2,1,4096]{3,1,2,0:T(2,128)(2,1)}) %all-gather.2.cloned.1.call-update) | async-done | bytes 4194320 | tf_op jit(solution)/shard_map/all_gather | solution.py:117
  657.3 9.2 %constant_dynamic-slice_fusion = bf16[256,1,1,4096]{3,1,2,0:T(2,128)(2,1)} fusion(bf16[256,2,1,4096]{3,1,2,0:T(2,128)(2,1)} %all-gather.2.cloned.1.call-done, s32[]{:T(128)S(6)} %select_n.273), kind=kLoop, calls=%fused_computation.114 | loop fusion | bytes 4194308 | tf_op jit(solution)/shard_map/jit(dynamic_index_in_dim)/dynamic_slice | solution.py:116
  666.6 6.2 fusion.18
  672.8 10.8 %fusion = bf16[256,1,4096]{2,0,1:T(8,128)(2,1)} fusion(bf16[1,448,4096]{2,1,0:T(8,128)(2,1)} %param.25, bf16[1,448,4096]{2,1,0:T(8,128)(2,1)} %param.24, bf16[256,1,1,4096]{3,1,2,0:T(2,128)(2,1)} %constant_dynamic-slice_fusion, f32[256,1,448]{0,2,1:T(8,128)S(1)} %fusion.18), kind=kOutput, calls=%fused_computation.12 | convolution fusion | flops 1880784896 | bytes 11993088 | tf_op jit(solution)/shard_map/nef,efd->ned/dot_general | solution.py:123
  684.2 1.6 broadcast_select_fusion
  685.8 4.8 all-to-all-start.2
  690.7 206.7 %reduce-scatter.5.cloned.1.call-done = bf16[8,1,4096]{2,0,1:T(8,128)(2,1)} async-done(((bf16[256,1,4096]{2,0,1:T(8,128)(2,1)}), bf16[8,1,4096]{2,0,1:T(8,128)(2,1)}) %reduce-scatter.5.cloned.1.call-update) | async-done | bytes 65552 | tf_op jit(solution)/shard_map/reduce_scatter | solution.py:122
  897.3 1.5 convert_element_type.130
  898.8 3.3 all-to-all-start.1
  903.4 1.3 reduce_sum.74
  904.7 1.5 all-to-all-done.1
  906.2 0.9 scatter_custom_fusion.2
  907.1 0.9 scatter_custom_fusion.3
  (67 shorter events, 8.6 us)
Async XLA Ops:
  7.2 122.9 %copy-start = (bf16[128,4096]{1,0:T(8,128)(2,1)S(1)}, bf16[128,4096]{1,0:T(8,128)(2,1)}, u32[]{:S(2)}) copy-start(bf16[128,4096]{1,0:T(8,128)(2,1)} %param.19) | copy-start | bytes 3145732
  11.2 13.2 %copy-start.6 = (s32[4,16]{1,0:T(4,128)S(1)}, s32[4,16]{1,0:T(4,128)}, u32[]{:S(2)}) copy-start(s32[4,16]{1,0:T(4,128)} %param.17) | copy-start | bytes 772
  11.2 13.3 %copy-start.8 = (s32[4]{0:T(128)S(1)}, s32[4]{0:T(128)}, u32[]{:S(2)}) copy-start(s32[4]{0:T(128)} %param.16) | copy-start | bytes 52
  11.2 108.4 %all-to-all-start = ((bf16[1,64,1,128,256]{4,3,2,0,1:T(8,128)(2,1)}), bf16[1,64,1,128,256]{4,3,2,0,1:T(8,128)(2,1)}, u32[]{:S(2)}, u32[]{:S(2)}) async-start(bf16[1,64,1,128,256]{4,3,2,0,1:T(8,128)(2,1)} %bitcast.171), calls=%async_computation | async-start | bytes 8388608 | tf_op jit(solution)/shard_map/all_to_all | solution.py:61
  24.4 327.6 %reduce-scatter.3.cloned.1.call-start = ((), (), s32[]{:S(2)}) async-start(), calls=%async_computation.5 | async-start | bytes 4325376 | tf_op jit(solution)/shard_map/reduce_scatter | solution.py:93
  119.6 5.0 copy-start.9
  124.6 3.7 copy-start.1
  130.0 3.3 copy-start.5
  130.0 222.0 %copy-start.3 = (bf16[16,4096]{1,0:T(8,128)(2,1)S(1)}, bf16[16,4096]{1,0:T(8,128)(2,1)}, u32[]{:S(2)}) copy-start(bf16[16,4096]{1,0:T(8,128)(2,1)} %param.13) | copy-start | bytes 393220
  133.2 220.7 %copy-start.4 = (f32[4096]{0:T(1024)S(1)}, f32[4096]{0:T(1024)}, u32[]{:S(2)}) copy-start(f32[4096]{0:T(1024)} %param.20) | copy-start | bytes 49156
  133.2 524.1 %all-gather.2.cloned.1.call-start = ((), (), s32[]{:S(2)}) async-start(), calls=%async_computation.6 | async-start | bytes 4259840 | tf_op jit(solution)/shard_map/all_gather | solution.py:117
  354.7 542.6 %reduce-scatter.5.cloned.1.call-start = ((), (), s32[]{:S(2)}) async-start(), calls=%async_computation.7 | async-start | bytes 2162688 | tf_op jit(solution)/shard_map/reduce_scatter | solution.py:122
  672.8 11.5 %copy-start.2 = (bf16[1,8,128,256]{3,2,1,0:T(8,128)(2,1)S(1)}, bf16[1,8,128,256]{3,2,1,0:T(8,128)(2,1)}, u32[]{:S(2)}) copy-start(bf16[1,8,128,256]{3,2,1,0:T(8,128)(2,1)} %param.15) | copy-start | bytes 1572868
  683.5 7.1 copy-start.7
  685.8 213.0 %all-to-all-start.2 = ((bf16[4,1,8,128,256]{4,3,2,1,0:T(8,128)(2,1)}), bf16[4,1,8,128,256]{4,3,2,1,0:T(8,128)(2,1)S(1)}, u32[]{:S(2)}, u32[]{:S(2)}) async-start(bf16[4,1,8,128,256]{4,3,2,1,0:T(8,128)(2,1)} %broadcast_select_fusion), calls=%async_computation.4 | async-start | bytes 4194304 | tf_op jit(solution)/shard_map/all_to_all | solution.py:18
  898.8 7.4 all-to-all-start.1
Sparse Core Ops, SparseCore 0:
  133.4 218.5 reduce-scatter.2
  354.8 302.4 all-gather.1
  683.7 213.5 reduce-scatter.4
where the time goes:
time: 916 us; the launch traced here: 915 us
  waiting for transfers between devices  820 us (90%)
  matrix products  24.2 us (3%)
  local copies, waits for them, and re-layouts  22.3 us (2%)
  starting transfers between devices  21.5 us (2%)
  between operations  14.6 us (2%)
  other arithmetic  12.5 us (1%)
    all_gather x1, waiting for transfers between devices, on_device(): lax.all_gather(by_expert, ('tp', 'dec'), axis=0, tiled=True)  302 us
    reduce_scatter x1, waiting for transfers between devices, on_device(): lax.psum_scatter(jnp.dot(attended, out_weight, preferred_element_type=jnp...  214 us
    reduce_scatter x1, waiting for transfers between devices, on_device(): lax.psum_scatter(jnp.einsum('nef,efd->ned', hidden, w_down, preferred_ele...  207 us
    all_to_all x1, waiting for transfers between devices, on_device(): lax.all_to_all(outgoing, ('tp', 'dec'), split_axis=1, concat_axis=0, tile...  95 us
  transfers between devices with their start and end apart: 6, of which 5 were waited for; matrix products, arithmetic and copies ran while one was open for 1% of the time, Pallas kernels for 0%

commit v1 on v0

--- a/solution.py
+++ b/solution.py
@@ -114,7 +114,15 @@
     width = normed.shape[2]
     by_expert = normed.reshape(routed_dev, dec_size, exp_dec, width)
     row_piece = lax.dynamic_index_in_dim(
-        lax.all_gather(by_expert, ("tp", "dec"), axis=0, tiled=True), dec_index, 1, keepdims=False
+        jnp.concatenate(
+            lax.all_to_all(
+                jnp.stack([by_expert] * lax.axis_size(("tp", "dec"))), ("tp", "dec"), 0, 0
+            ),
+            axis=0,
+        ),
+        dec_index,
+        1,
+        keepdims=False,
     )
     gate_part = jnp.einsum("ned,efd->nef", row_piece, w_gate, preferred_element_type=jnp.float32)
     up_part = jnp.einsum("ned,efd->nef", row_piece, w_up, preferred_element_type=jnp.float32)

time: 916 us -> 717 us (0.78)
  waiting for transfers between devices: 820 us -> 608 us
    all_gather x1 -> x0, waiting for transfers between devices: 302 us -> none  [on_device(): lax.all_gather(by_expert, ('tp', 'dec'), axis=0, tiled=True)]
    all_to_all x0 -> x1, waiting for transfers between devices: none -> 90 us  [on_device(): lax.all_to_all(jnp.stack([by_expert] * lax.axis_size(('tp', 'dec'))), ('t...]
where the time goes in v1:
time: 717 us; the launch traced here: 716 us
  waiting for transfers between devices  608 us (85%)
  starting transfers between devices  29.7 us (4%)
  local copies, waits for them, and re-layouts  28.2 us (4%)
  matrix products  23.1 us (3%)
  between operations  15 us (2%)
  other arithmetic  11.9 us (2%)
    reduce_scatter x1, waiting for transfers between devices, on_device(): lax.psum_scatter(jnp.dot(attended, out_weight, preferred_element_type=jnp...  214 us
    reduce_scatter x1, waiting for transfers between devices, on_device(): lax.psum_scatter(jnp.einsum('nef,efd->ned', hidden, w_down, preferred_ele...  207 us
    all_to_all x1, waiting for transfers between devices, on_device(): lax.all_to_all(outgoing, ('tp', 'dec'), split_axis=1, concat_axis=0, tile...  95 us
    all_to_all x1, waiting for transfers between devices, on_device(): lax.all_to_all(jnp.stack([by_expert] * lax.axis_size(('tp', 'dec'))), ('t...  90 us
  transfers between devices with their start and end apart: 6, of which 5 were waited for; matrix products, arithmetic and copies ran while one was open for 1% of the time, Pallas kernels for 0%

profile of v1, /device:TPU:4, one launch (start us, length us, event | category | flops | bytes accessed | tf_op | source)
XLA Modules:
  0.0 715.9 jit_solution(16186729135136765823)
XLA Ops:
  7.2 1.4 broadcast_in_dim.77
  8.5 2.7 broadcast_in_dim.79
  11.2 13.1 %all-to-all-start = ((bf16[1,64,1,128,256]{4,3,2,0,1:T(8,128)(2,1)}), bf16[1,64,1,128,256]{4,3,2,0,1:T(8,128)(2,1)}, u32[]{:S(2)}, u32[]{:S(2)}) async-start(bf16[1,64,1,128,256]{4,3,2,0,1:T(8,128)(2,1)} %bitcast.177), calls=%async_computation | async-start | bytes 8388608 | tf_op jit(solution)/shard_map/all_to_all | solution.py:61
  24.6 95.0 %all-to-all-done = bf16[1,64,1,128,256]{4,3,2,0,1:T(8,128)(2,1)} async-done(((bf16[1,64,1,128,256]{4,3,2,0,1:T(8,128)(2,1)}), bf16[1,64,1,128,256]{4,3,2,0,1:T(8,128)(2,1)}, u32[]{:S(2)}, u32[]{:S(2)}) %all-to-all-start) | async-done | bytes 4194336 | tf_op jit(solution)/shard_map/all_to_all | solution.py:61
  119.6 5.0 gather_fusion
  124.6 2.4 fusion.6
  127.0 1.3 fusion.7
  128.3 1.7 fusion.51
  130.1 3.2 convolution_convert_fusion
  137.6 214.4 %reduce-scatter.3.cloned.1.call-done = bf16[16,4096]{1,0:T(8,128)(2,1)} async-done(((bf16[512,4096]{1,0:T(8,128)(2,1)}), bf16[16,4096]{1,0:T(8,128)(2,1)}) %reduce-scatter.3.cloned.1.call-update) | async-done | bytes 131088 | tf_op jit(solution)/shard_map/reduce_scatter | solution.py:93
  353.9 6.2 stack.17
  360.1 8.2 %all-to-all-start.1 = ((bf16[64,4,2,1,4096]{4,2,1,3,0:T(2,128)(2,1)}), bf16[64,4,2,1,4096]{4,2,1,3,0:T(2,128)(2,1)}, u32[]{:S(2)}, u32[]{:S(2)}) async-start(bf16[64,4,2,1,4096]{4,2,1,3,0:T(2,128)(2,1)} %stack.17), calls=%async_computation.2 | async-start | bytes 8388608 | tf_op jit(solution)/shard_map/all_to_all | solution.py:118
  368.6 90.0 %all-to-all-done.1 = bf16[64,4,2,1,4096]{4,2,1,3,0:T(2,128)(2,1)} async-done(((bf16[64,4,2,1,4096]{4,2,1,3,0:T(2,128)(2,1)}), bf16[64,4,2,1,4096]{4,2,1,3,0:T(2,128)(2,1)}, u32[]{:S(2)}, u32[]{:S(2)}) %all-to-all-start.1) | async-done | bytes 4194336 | tf_op jit(solution)/shard_map/all_to_all | solution.py:118
  458.6 7.0 constant_dynamic-slice_fusion
  465.6 1.9 copy-done.2
  467.5 5.1 fusion.20
  472.6 10.8 %fusion = bf16[256,1,4096]{2,0,1:T(8,128)(2,1)} fusion(bf16[1,448,4096]{2,1,0:T(8,128)(2,1)} %param.25, bf16[1,448,4096]{2,1,0:T(8,128)(2,1)} %param.24, bf16[256,1,1,4096]{3,1,0,2:T(2,128)(2,1)} %copy-done.2, f32[256,1,448]{0,2,1:T(8,128)S(1)} %fusion.20), kind=kOutput, calls=%fused_computation.12 | convolution fusion | flops 1880784896 | bytes 11993088 | tf_op jit(solution)/shard_map/nef,efd->ned/dot_general | solution.py:131
  484.1 1.6 broadcast_select_fusion
  485.7 4.8 all-to-all-start.3
  490.5 207.2 %reduce-scatter.5.cloned.1.call-done = bf16[8,1,4096]{2,0,1:T(8,128)(2,1)} async-done(((bf16[256,1,4096]{2,0,1:T(8,128)(2,1)}), bf16[8,1,4096]{2,0,1:T(8,128)(2,1)}) %reduce-scatter.5.cloned.1.call-update) | async-done | bytes 65552 | tf_op jit(solution)/shard_map/reduce_scatter | solution.py:130
  697.7 1.5 convert_element_type.128
  699.2 3.3 all-to-all-start.2
  703.8 1.3 reduce_sum.74
  705.0 1.5 all-to-all-done.2
  (68 shorter events, 10.5 us)
Async XLA Ops:
  7.2 122.9 %copy-start = (bf16[128,4096]{1,0:T(8,128)(2,1)S(1)}, bf16[128,4096]{1,0:T(8,128)(2,1)}, u32[]{:S(2)}) copy-start(bf16[128,4096]{1,0:T(8,128)(2,1)} %param.19) | copy-start | bytes 3145732
  11.2 13.2 %copy-start.7 = (s32[4,16]{1,0:T(4,128)S(1)}, s32[4,16]{1,0:T(4,128)}, u32[]{:S(2)}) copy-start(s32[4,16]{1,0:T(4,128)} %param.17) | copy-start | bytes 772
  11.2 13.3 %copy-start.9 = (s32[4]{0:T(128)S(1)}, s32[4]{0:T(128)}, u32[]{:S(2)}) copy-start(s32[4]{0:T(128)} %param.16) | copy-start | bytes 52
  11.2 108.4 %all-to-all-start = ((bf16[1,64,1,128,256]{4,3,2,0,1:T(8,128)(2,1)}), bf16[1,64,1,128,256]{4,3,2,0,1:T(8,128)(2,1)}, u32[]{:S(2)}, u32[]{:S(2)}) async-start(bf16[1,64,1,128,256]{4,3,2,0,1:T(8,128)(2,1)} %bitcast.177), calls=%async_computation | async-start | bytes 8388608 | tf_op jit(solution)/shard_map/all_to_all | solution.py:61
  24.4 327.6 %reduce-scatter.3.cloned.1.call-start = ((), (), s32[]{:S(2)}) async-start(), calls=%async_computation.6 | async-start | bytes 4325376 | tf_op jit(solution)/shard_map/reduce_scatter | solution.py:93
  119.6 5.0 copy-start.10
  124.6 3.7 copy-start.1
  130.0 3.2 copy-start.6
  130.0 221.9 %copy-start.4 = (bf16[16,4096]{1,0:T(8,128)(2,1)S(1)}, bf16[16,4096]{1,0:T(8,128)(2,1)}, u32[]{:S(2)}) copy-start(bf16[16,4096]{1,0:T(8,128)(2,1)} %param.13) | copy-start | bytes 393220
  133.2 220.6 %copy-start.5 = (f32[4096]{0:T(1024)S(1)}, f32[4096]{0:T(1024)}, u32[]{:S(2)}) copy-start(f32[4096]{0:T(1024)} %param.20) | copy-start | bytes 49156
  360.1 98.4 %all-to-all-start.1 = ((bf16[64,4,2,1,4096]{4,2,1,3,0:T(2,128)(2,1)}), bf16[64,4,2,1,4096]{4,2,1,3,0:T(2,128)(2,1)}, u32[]{:S(2)}, u32[]{:S(2)}) async-start(bf16[64,4,2,1,4096]{4,2,1,3,0:T(2,128)(2,1)} %stack.17), calls=%async_computation.2 | async-start | bytes 8388608 | tf_op jit(solution)/shard_map/all_to_all | solution.py:118
  368.3 329.3 %reduce-scatter.5.cloned.1.call-start = ((), (), s32[]{:S(2)}) async-start(), calls=%async_computation.7 | async-start | bytes 2162688 | tf_op jit(solution)/shard_map/reduce_scatter | solution.py:130
  465.6 1.9 copy-start.2
  472.6 11.5 %copy-start.3 = (bf16[1,8,128,256]{3,2,1,0:T(8,128)(2,1)S(1)}, bf16[1,8,128,256]{3,2,1,0:T(8,128)(2,1)}, u32[]{:S(2)}) copy-start(bf16[1,8,128,256]{3,2,1,0:T(8,128)(2,1)} %param.15) | copy-start | bytes 1572868
  483.4 7.1 copy-start.8
  485.7 213.5 %all-to-all-start.3 = ((bf16[4,1,8,128,256]{4,3,2,1,0:T(8,128)(2,1)}), bf16[4,1,8,128,256]{4,3,2,1,0:T(8,128)(2,1)S(1)}, u32[]{:S(2)}, u32[]{:S(2)}) async-start(bf16[4,1,8,128,256]{4,3,2,1,0:T(8,128)(2,1)} %broadcast_select_fusion), calls=%async_computation.5 | async-start | bytes 4194304 | tf_op jit(solution)/shard_map/all_to_all | solution.py:18
  699.2 7.4 %all-to-all-start.2 = ((bf16[2,4,1,4096]{3,1,2,0:T(4,128)(2,1)}), bf16[2,4,1,4096]{3,1,2,0:T(4,128)(2,1)S(1)}, u32[]{:S(2)}, u32[]{:S(2)}) async-start(bf16[2,4,1,4096]{3,1,2,0:T(4,128)(2,1)} %bitcast.41), calls=%async_computation.4 | async-start | bytes 131072 | tf_op jit(solution)/shard_map/all_to_all | solution.py:140
Sparse Core Ops, SparseCore 0:
  133.4 218.5 reduce-scatter.2
  483.5 214.0 reduce-scatter.4
